TPU v7x, 256 devices: a whole 4x4x8 slice. The times are simulated.
256 devices in a mesh: dp: 2 (over core), seq: 8 (over z), expert: 16 (over y, x).
Axes of the slice: x: 4, y: 4, z: 8, core: 2. Of those that a mesh axis runs over, the one named last changes fastest.
Arguments:
- tokens: bfloat16 [16384, 2048], P(('dp', 'seq')), may hold values from -6 to 6
- phi: bfloat16 [2048, 32], P(None, 'expert'), may hold values from -40 to 40
- w_in: bfloat16 [32, 2048, 8192], P('expert', None, ('dp', 'seq')), may hold values from -1 to 1
- w_out: bfloat16 [32, 8192, 2048], P('expert', ('dp', 'seq')), may hold values from -0.25 to 0.25
Outputs:
- mixed: bfloat16 [16384, 2048], P(('dp', 'seq', 'expert'))
All inputs are finite; a program needn't handle non-finite values.
Results may differ from a plain program's by a relative error of at most 0.0068.
Values may be sent and summed in bfloat16 or wider, within the bound.
A program may use at most 64 MiB of HBM per device.

v0:
```python
import jax
import jax.numpy as jnp
from jax import lax
from jax.sharding import PartitionSpec as P


def on_device(tokens, phi, w_in, w_out):
    n_expert = lax.axis_size("expert")
    rows_out = tokens.shape[0] // n_expert
    phi_all = lax.all_gather(phi, "expert", axis=1, tiled=True)
    logits = lax.dot_general(
        phi, tokens, (((0,), (1,)), ((), ())), preferred_element_type=jnp.float32
    )
    slot_max = lax.pmax(jnp.max(logits, axis=1), "seq")
    spread = jnp.exp(logits - slot_max[:, None])
    numerator = jnp.dot(spread.astype(jnp.bfloat16), tokens, preferred_element_type=jnp.float32)
    denominator = jnp.sum(spread, axis=1)
    numer_seq, denom_seq = lax.psum((numerator, denominator), "seq")
    own_slots = (numer_seq / denom_seq[:, None]).astype(jnp.bfloat16)
    slot_in = lax.all_gather(own_slots[None], "dp", axis=0, tiled=True)
    hidden = jax.nn.gelu(
        jnp.einsum("ced,edf->cef", slot_in, w_in, preferred_element_type=jnp.float32),
        approximate=True,
    ).astype(jnp.bfloat16)
    partial_value = jnp.einsum("cef,efd->ced", hidden, w_out, preferred_element_type=jnp.float32)
    totals = lax.psum(partial_value, ("dp", "seq"))
    summed = lax.dynamic_index_in_dim(totals, lax.axis_index("dp"), 0, keepdims=False)
    slot_out = lax.all_gather(summed.astype(jnp.bfloat16), "expert", axis=0, tiled=True)
    rows = lax.dynamic_slice_in_dim(tokens, lax.axis_index("expert") * rows_out, rows_out, 0)
    row_logits = lax.dot_general(
        phi_all, rows, (((0,), (1,)), ((), ())), preferred_element_type=jnp.float32
    )
    row_max = jnp.max(row_logits, axis=0)
    combine_weights = jnp.exp(row_logits - row_max[None, :])
    mixed_numer = lax.dot_general(
        combine_weights.astype(jnp.bfloat16),
        slot_out,
        (((0,), (0,)), ((), ())),
        preferred_element_type=jnp.float32,
    )
    mixed_denom = jnp.sum(combine_weights, axis=0)
    return (mixed_numer / mixed_denom[:, None]).astype(jnp.bfloat16)


def solution(mesh):
    placed = (
        P(("dp", "seq"), None),
        P(None, "expert"),
        P("expert", None, ("dp", "seq")),
        P("expert", ("dp", "seq"), None),
    )
    return jax.shard_map(
        on_device,
        mesh=mesh,
        in_specs=placed,
        out_specs=P(("dp", "seq", "expert"), None),
        check_vma=False,
    )
```

profile of v0, /device:TPU:32, one launch (start us, length us, event | category | flops | bytes accessed | tf_op | source)
XLA Modules:
  0.0 159.4 jit_solution(6288700102996713554)
XLA Ops:
  0.0 3.5 %fusion.39 = (f32[2]{0:T(128)S(1)}, f32[2,1024]{1,0:T(2,128)S(1)}) fusion(bf16[2048,2]{0,1:T(2,128)(2,1)} %param.5, bf16[1024,2048]{1,0:T(8,128)(2,1)} %param.4), kind=kOutput, calls=%fused_computation.39 | convolution fusion | flops 8390654 | bytes 4210696 | tf_op jit(solution)/shard_map/dot_general | solution.py:11
  3.5 17.9 %pmax.7 = f32[2]{0:T(128)S(1)} all-reduce(f32[2]{0:T(128)S(1)} %get-tuple-element.9), channel_id=1, replica_groups=mesh['dp'=2,'seq'=8,'expert'=16] {'seq'}, use_global_device_ids=true, to_apply=%region_2.0 | all-reduce | flops 2 | bytes 16 | tf_op jit(solution)/shard_map/pmax | solution.py:14
  21.4 0.2 fusion.25
  21.6 2.9 %fusion.27 = f32[2,2048]{1,0:T(2,128)S(1)} fusion(bf16[1024,2048]{1,0:T(8,128)(2,1)} %param.4, f32[2,1024]{1,0:T(2,128)S(1)} %get-tuple-element.10, f32[2]{0:T(128)S(1)} %pmax.7), kind=kOutput, calls=%fused_computation.28 | convolution fusion | flops 8392704 | bytes 4218888 | tf_op jit(solution)/shard_map/dot_general | solution.py:16
  24.5 27.9 %all-reduce = (f32[2,2048]{1,0:T(2,128)S(1)}, f32[2]{0:T(128)S(1)}) all-reduce(f32[2,2048]{1,0:T(2,128)S(1)} %fusion.27, f32[2]{0:T(128)S(1)} %fusion.25), channel_id=1, replica_groups=mesh['dp'=2,'seq'=8,'expert'=16] {'seq'}, use_global_device_ids=true, to_apply=%region_3.0 | all-reduce | flops 4098 | bytes 32784 | tf_op jit(solution)/shard_map/psum | solution.py:18
  52.4 0.1 fusion.24
  52.5 1.8 %all-gather.3 = bf16[2,2,2048]{2,1,0:T(2,128)(2,1)S(1)} all-gather(bf16[1,2,2048]{2,1,0:T(2,128)(2,1)S(1)} %fusion.24), channel_id=2, replica_groups=mesh['dp'=2,'seq'=8,'expert'=16] {'dp'}, dimensions={0}, use_global_device_ids=true | all-gather | bytes 24576 | tf_op jit(solution)/shard_map/all_gather | solution.py:20
  54.3 0.0 copy-start
  54.3 4.7 %convolution_bitcast_fusion = f32[2,2,2048]{2,0,1:T(2,128)S(1)} fusion(bf16[2,512,2048]{2,1,0:T(8,128)(2,1)} %param.7, bf16[2,2048,512]{2,1,0:T(8,128)(2,1)} %param.6, bf16[2,2,2048]{2,1,0:T(2,128)(2,1)S(1)} %all-gather.3), kind=kOutput, calls=%fused_computation.2 | convolution fusion | flops 16795648 | bytes 8437760 | tf_op jit(solution)/shard_map/cef,efd->ced/dot_general | solution.py:25
  59.0 51.1 %psum.23 = bf16[2,2,2048]{2,0,1:T(2,128)(2,1)S(1)} all-reduce(f32[2,2,2048]{2,0,1:T(2,128)S(1)} %convolution_bitcast_fusion), channel_id=1, replica_groups=mesh['dp'=2,'seq'=8,'expert'=16] {'dp','seq'}, use_global_device_ids=true, to_apply=%region_6.7 | all-reduce | flops 8192 | bytes 49152 | tf_op jit(solution)/shard_map/psum | solution.py:26
  110.1 0.0 copy-done
  110.1 24.0 %all-gather.2 = bf16[16,2,2048]{2,1,0:T(2,128)(2,1)S(1)} all-gather(bf16[1,2,2048]{2,1,0:T(2,128)(2,1)S(1)} %bitcast.24), channel_id=1, replica_groups=mesh['dp'=2,'seq'=8,'expert'=16] {'expert'}, dimensions={0}, use_global_device_ids=true | all-gather | bytes 139264 | tf_op jit(solution)/shard_map/all_gather | solution.py:10
  134.1 0.1 reshape.8
  134.1 1.2 fusion.38
  135.3 23.1 %all-gather.1 = bf16[1,32,2048]{2,0,1:T(2,128)(2,1)S(1)} all-gather(bf16[1,2,2048]{2,0,1:T(2,128)(2,1)S(1)} %dynamic-slice_convert_fusion), channel_id=3, replica_groups=mesh['dp'=2,'seq'=8,'expert'=16] {'expert'}, dimensions={1}, use_global_device_ids=true | all-gather | bytes 139264 | tf_op jit(solution)/shard_map/all_gather | solution.py:28
  158.4 1.0 fusion
  (2 shorter events, 0.1 us)
Async XLA Ops:
  54.3 55.8 %copy-start = (bf16[2048,2]{0,1:T(2,128)(2,1)S(1)}, bf16[2048,2]{0,1:T(2,128)(2,1)}, u32[]{:S(2)}) copy-start(bf16[2048,2]{0,1:T(2,128)(2,1)} %param.5) | copy-start | bytes 24580
where the time goes:
time: 160 us; the launch traced here: 159 us
  blocking collectives  146 us (91%)
  matrix products  13.2 us (8%)
    psum x1, blocking collectives, on_device(): totals = lax.psum(partial_value, ('dp', 'seq'))  51.1 us
    psum x1, blocking collectives, on_device(): numer_seq, denom_seq = lax.psum((numerator, denominator), 'seq')  27.9 us
    all_gather x1, blocking collectives, on_device(): phi_all = lax.all_gather(phi, 'expert', axis=1, tiled=True)  24 us
    all_gather x1, blocking collectives, on_device(): lax.all_gather(summed.astype(jnp.bfloat16), 'expert', axis=0, tiled=True)  23.1 us
    pmax x1, blocking collectives, on_device(): slot_max = lax.pmax(jnp.max(logits, axis=1), 'seq')  17.9 us
    dot_general x1, matrix products, on_device(): jnp.einsum('cef,efd->ced', hidden, w_out, preferred_element_type=jnp.floa...  4.66 us
    dot_general x1, matrix products, on_device(): lax.dot_general(phi, tokens, (((0,), (1,)), ((), ())), preferred_element_...  3.5 us

commit v1 on v0

--- a/solution.py
+++ b/solution.py
@@ -7,7 +7,28 @@
 def on_device(tokens, phi, w_in, w_out):
     n_expert = lax.axis_size("expert")
     rows_out = tokens.shape[0] // n_expert
-    phi_all = lax.all_gather(phi, "expert", axis=1, tiled=True)
+    part_now = jax.lax.axis_size("expert")
+    after = jax.lax.axis_index("expert")
+    view_out, carry_out, d_next = (part_now, after, phi.shape[1])
+    a_next = jnp.zeros(
+        [dev_i * view_out if pp == 1 else dev_i for pp, dev_i in enumerate(phi.shape)], phi.dtype
+    )
+    phi_all = lax.dynamic_update_slice_in_dim(a_next, phi, carry_out * d_next, axis=1)
+    z_new = latest = phi
+    for idx in [*range(1, view_out // 2 + 1)]:
+        z_new = jax.lax.ppermute(
+            z_new, "expert", [(pp, (pp + 1) % view_out) for pp in range(view_out)]
+        )
+        phi_all = lax.dynamic_update_slice_in_dim(
+            phi_all, z_new, (carry_out - idx) % view_out * d_next, axis=1
+        )
+        if 2 * idx < view_out:
+            latest = jax.lax.ppermute(
+                latest, "expert", [(pp, (pp - 1) % view_out) for pp in range(view_out)]
+            )
+            phi_all = lax.dynamic_update_slice_in_dim(
+                phi_all, latest, (carry_out + idx) % view_out * d_next, axis=1
+            )
     logits = lax.dot_general(
         phi, tokens, (((0,), (1,)), ((), ())), preferred_element_type=jnp.float32
     )

time: 160 us -> 190 us (1.19)
  starting transfers between devices: 0 us -> 37.5 us
  blocking collectives: 146 us -> 121 us
  waiting for transfers between devices: 0 us -> 16.4 us
    ppermute x0 -> x15, starting transfers between devices: none -> 37.5 us  [the longest x7 35.8 us: on_device(): jax.lax.ppermute(latest, 'expert', [(pp, (pp - 1) % view_out) for pp in r...]
    all_gather x1 -> x0, blocking collectives: 24 us -> none  [on_device(): phi_all = lax.all_gather(phi, 'expert', axis=1, tiled=True)]
    ppermute x0 -> x15, waiting for transfers between devices: none -> 16.4 us  [the longest x8 16.4 us: on_device(): jax.lax.ppermute(z_new, 'expert', [(pp, (pp + 1) % view_out) for pp in ra...]
  transfers between devices with their start and end apart: 0 -> 15, of which waited for: 0 -> 7; matrix products, arithmetic and copies ran while one was open for 0% -> 6% of each run, Pallas kernels for 0% -> 0%
where the time goes in v1:
time: 190 us; the launch traced here: 189 us
  blocking collectives  121 us (64%)
  starting transfers between devices  37.5 us (20%)
  waiting for transfers between devices  16.4 us (9%)
  matrix products  13.2 us (7%)
    psum x1, blocking collectives, on_device(): totals = lax.psum(partial_value, ('dp', 'seq'))  51.1 us
    ppermute x7, starting transfers between devices, on_device(): jax.lax.ppermute(latest, 'expert', [(pp, (pp - 1) % view_out) for pp in r...  35.8 us
    psum x1, blocking collectives, on_device(): numer_seq, denom_seq = lax.psum((numerator, denominator), 'seq')  27.9 us
    all_gather x1, blocking collectives, on_device(): lax.all_gather(summed.astype(jnp.bfloat16), 'expert', axis=0, tiled=True)  22.6 us
    pmax x1, blocking collectives, on_device(): slot_max = lax.pmax(jnp.max(logits, axis=1), 'seq')  17.9 us
    ppermute x8, waiting for transfers between devices, on_device(): jax.lax.ppermute(z_new, 'expert', [(pp, (pp + 1) % view_out) for pp in ra...  16.4 us
    dot_general x1, matrix products, on_device(): jnp.einsum('cef,efd->ced', hidden, w_out, preferred_element_type=jnp.floa...  4.66 us
  transfers between devices with their start and end apart: 15, of which 7 were waited for; matrix products, arithmetic and copies ran while one was open for 6% of the time, Pallas kernels for 0%

profile of v1, /device:TPU:32, one launch (start us, length us, event | category | flops | bytes accessed | tf_op | source)
XLA Modules:
  0.0 189.3 jit_solution(12360647325249847426)
XLA Ops:
  0.0 1.5 collective-permute-start
  1.5 3.9 %collective-permute-start.1 = (bf16[2048,2]{0,1:T(2,128)(2,1)}, bf16[2048,2]{0,1:T(2,128)(2,1)S(1)}, u32[]{:S(2)}, u32[]{:S(2)}) collective-permute-start(bf16[2048,2]{0,1:T(2,128)(2,1)} %param.5), channel_id=1, source_target_pairs={{0,15},{1,0},{2,1},{3,2},{4,3},{5,4},{6,5},{7,6},{8,7},{9,8},{10,9... | collective-permute-start | bytes 24584 | tf_op jit(solution)/shard_map/ppermute | solution.py:26
  5.3 3.5 %fusion.39 = (f32[2]{0:T(128)S(1)}, f32[2,1024]{1,0:T(2,128)S(1)}) fusion(bf16[2048,2]{0,1:T(2,128)(2,1)} %param.5, bf16[1024,2048]{1,0:T(8,128)(2,1)} %param.4), kind=kOutput, calls=%fused_computation.55 | convolution fusion | flops 8390654 | bytes 4210696 | tf_op jit(solution)/shard_map/dot_general | solution.py:32
  8.9 17.9 %pmax.7 = f32[2]{0:T(128)S(1)} all-reduce(f32[2]{0:T(128)S(1)} %get-tuple-element.9), channel_id=1, replica_groups=mesh['dp'=2,'seq'=8,'expert'=16] {'seq'}, use_global_device_ids=true, to_apply=%region_2.3 | all-reduce | flops 2 | bytes 16 | tf_op jit(solution)/shard_map/pmax | solution.py:35
  26.7 0.2 fusion.26
  26.9 2.9 %fusion.28 = f32[2,2048]{1,0:T(2,128)S(1)} fusion(bf16[1024,2048]{1,0:T(8,128)(2,1)} %param.4, f32[2,1024]{1,0:T(2,128)S(1)} %get-tuple-element.10, f32[2]{0:T(128)S(1)} %pmax.7), kind=kOutput, calls=%fused_computation.45 | convolution fusion | flops 8392704 | bytes 4218888 | tf_op jit(solution)/shard_map/dot_general | solution.py:37
  29.8 27.9 %all-reduce = (f32[2,2048]{1,0:T(2,128)S(1)}, f32[2]{0:T(128)S(1)}) all-reduce(f32[2,2048]{1,0:T(2,128)S(1)} %fusion.28, f32[2]{0:T(128)S(1)} %fusion.26), channel_id=1, replica_groups=mesh['dp'=2,'seq'=8,'expert'=16] {'seq'}, use_global_device_ids=true, to_apply=%region_3.4 | all-reduce | flops 4098 | bytes 32784 | tf_op jit(solution)/shard_map/psum | solution.py:39
  57.7 0.1 fusion.24
  57.8 1.8 all-gather.2
  59.6 0.0 copy-start
  59.6 4.7 %convolution_bitcast_fusion = f32[2,2,2048]{2,0,1:T(2,128)S(1)} fusion(bf16[2,512,2048]{2,1,0:T(8,128)(2,1)} %param.7, bf16[2,2048,512]{2,1,0:T(8,128)(2,1)} %param.6, bf16[2,2,2048]{2,1,0:T(2,128)(2,1)S(1)} %all-gather.2), kind=kOutput, calls=%fused_computation.2 | convolution fusion | flops 16795648 | bytes 8437760 | tf_op jit(solution)/shard_map/cef,efd->ced/dot_general | solution.py:46
  64.3 51.1 %psum.23 = bf16[2,2,2048]{2,0,1:T(2,128)(2,1)S(1)} all-reduce(f32[2,2,2048]{2,0,1:T(2,128)S(1)} %convolution_bitcast_fusion), channel_id=1, replica_groups=mesh['dp'=2,'seq'=8,'expert'=16] {'dp','seq'}, use_global_device_ids=true, to_apply=%region_6.7 | all-reduce | flops 8192 | bytes 49152 | tf_op jit(solution)/shard_map/psum | solution.py:47
  115.4 22.6 %all-gather.1 = bf16[1,32,2048]{2,0,1:T(2,128)(2,1)S(1)} all-gather(bf16[1,2,2048]{2,0,1:T(2,128)(2,1)S(1)} %dynamic-slice_convert_fusion), channel_id=3, replica_groups=mesh['dp'=2,'seq'=8,'expert'=16] {'expert'}, dimensions={1}, use_global_device_ids=true | all-gather | bytes 139264 | tf_op jit(solution)/shard_map/all_gather | solution.py:49
  138.0 0.0 copy-done
  138.2 0.0 collective-permute-done
  138.2 0.2 collective-permute-start.2
  138.4 0.0 collective-permute-done.1
  138.5 5.2 %collective-permute-start.3 = (bf16[2048,2]{0,1:T(2,128)(2,1)S(1)}, bf16[2048,2]{0,1:T(2,128)(2,1)S(1)}, u32[]{:S(2)}, u32[]{:S(2)}) collective-permute-start(bf16[2048,2]{0,1:T(2,128)(2,1)S(1)} %collective-permute-done.1), channel_id=1, source_target_pairs={{0,15},{1,0},{2,1},{3,2},{4,3},{5,4},{6,5},{7,6},{8,7},{9,8},{10,9... | collective-permute-start | bytes 24584 | tf_op jit(solution)/shard_map/ppermute | solution.py:26
  143.7 1.6 collective-permute-done.2
  145.3 0.0 collective-permute-start.4
  145.3 0.0 collective-permute-done.3
  145.3 5.3 %collective-permute-start.5 = (bf16[2048,2]{0,1:T(2,128)(2,1)S(1)}, bf16[2048,2]{0,1:T(2,128)(2,1)S(1)}, u32[]{:S(2)}, u32[]{:S(2)}) collective-permute-start(bf16[2048,2]{0,1:T(2,128)(2,1)S(1)} %collective-permute-done.3), channel_id=1, source_target_pairs={{0,15},{1,0},{2,1},{3,2},{4,3},{5,4},{6,5},{7,6},{8,7},{9,8},{10,9... | collective-permute-start | bytes 24584 | tf_op jit(solution)/shard_map/ppermute | solution.py:26
  150.7 1.6 collective-permute-done.4
  152.3 0.0 collective-permute-start.6
  152.3 0.0 collective-permute-done.5
  152.3 5.3 %collective-permute-start.7 = (bf16[2048,2]{0,1:T(2,128)(2,1)S(1)}, bf16[2048,2]{0,1:T(2,128)(2,1)S(1)}, u32[]{:S(2)}, u32[]{:S(2)}) collective-permute-start(bf16[2048,2]{0,1:T(2,128)(2,1)S(1)} %collective-permute-done.5), channel_id=1, source_target_pairs={{0,15},{1,0},{2,1},{3,2},{4,3},{5,4},{6,5},{7,6},{8,7},{9,8},{10,9... | collective-permute-start | bytes 24584 | tf_op jit(solution)/shard_map/ppermute | solution.py:26
  157.7 1.6 collective-permute-done.6
  159.2 0.0 collective-permute-start.8
  159.2 0.0 collective-permute-done.7
  159.2 5.3 %collective-permute-start.9 = (bf16[2048,2]{0,1:T(2,128)(2,1)S(1)}, bf16[2048,2]{0,1:T(2,128)(2,1)S(1)}, u32[]{:S(2)}, u32[]{:S(2)}) collective-permute-start(bf16[2048,2]{0,1:T(2,128)(2,1)S(1)} %collective-permute-done.7), channel_id=1, source_target_pairs={{0,15},{1,0},{2,1},{3,2},{4,3},{5,4},{6,5},{7,6},{8,7},{9,8},{10,9... | collective-permute-start | bytes 24584 | tf_op jit(solution)/shard_map/ppermute | solution.py:26
  164.6 1.6 collective-permute-done.8
  166.2 0.0 collective-permute-start.10
  166.2 0.0 collective-permute-done.9
  166.2 5.3 %collective-permute-start.11 = (bf16[2048,2]{0,1:T(2,128)(2,1)S(1)}, bf16[2048,2]{0,1:T(2,128)(2,1)S(1)}, u32[]{:S(2)}, u32[]{:S(2)}) collective-permute-start(bf16[2048,2]{0,1:T(2,128)(2,1)S(1)} %collective-permute-done.9), channel_id=1, source_target_pairs={{0,15},{1,0},{2,1},{3,2},{4,3},{5,4},{6,5},{7,6},{8,7},{9,8},{10,9... | collective-permute-start | bytes 24584 | tf_op jit(solution)/shard_map/ppermute | solution.py:26
  171.6 1.6 collective-permute-done.10
  173.2 0.0 collective-permute-start.12
  173.2 0.0 collective-permute-done.11
  173.2 5.3 %collective-permute-start.13 = (bf16[2048,2]{0,1:T(2,128)(2,1)S(1)}, bf16[2048,2]{0,1:T(2,128)(2,1)S(1)}, u32[]{:S(2)}, u32[]{:S(2)}) collective-permute-start(bf16[2048,2]{0,1:T(2,128)(2,1)S(1)} %collective-permute-done.11), channel_id=1, source_target_pairs={{0,15},{1,0},{2,1},{3,2},{4,3},{5,4},{6,5},{7,6},{8,7},{9,8},{10,9... | collective-permute-start | bytes 24584 | tf_op jit(solution)/shard_map/ppermute | solution.py:26
  178.6 1.6 collective-permute-done.12
  180.2 0.0 collective-permute-start.14
  180.2 0.0 collective-permute-done.13
  180.2 6.9 %collective-permute-done.14 = bf16[2048,2]{0,1:T(2,128)(2,1)S(1)} collective-permute-done((bf16[2048,2]{0,1:T(2,128)(2,1)S(1)}, bf16[2048,2]{0,1:T(2,128)(2,1)S(1)}, u32[]{:S(2)}, u32[]{:S(2)}) %collective-permute-start.14) | collective-permute-done | bytes 8224 | tf_op jit(solution)/shard_map/ppermute | solution.py:19
  187.1 1.2 fusion.38
  188.3 1.0 fusion
  (19 shorter events, 0.4 us)
Async XLA Ops:
  0.0 138.2 %collective-permute-start = (bf16[2048,2]{0,1:T(2,128)(2,1)}, bf16[2048,2]{0,1:T(2,128)(2,1)S(1)}, u32[]{:S(2)}, u32[]{:S(2)}) collective-permute-start(bf16[2048,2]{0,1:T(2,128)(2,1)} %param.5), channel_id=1, source_target_pairs={{0,1},{1,2},{2,3},{3,4},{4,5},{5,6},{6,7},{7,8},{8,9},{9,10},{10,1... | collective-permute-start | bytes 24584 | tf_op jit(solution)/shard_map/ppermute | solution.py:19
  1.5 137.0 %collective-permute-start.1 = (bf16[2048,2]{0,1:T(2,128)(2,1)}, bf16[2048,2]{0,1:T(2,128)(2,1)S(1)}, u32[]{:S(2)}, u32[]{:S(2)}) collective-permute-start(bf16[2048,2]{0,1:T(2,128)(2,1)} %param.5), channel_id=1, source_target_pairs={{0,15},{1,0},{2,1},{3,2},{4,3},{5,4},{6,5},{7,6},{8,7},{9,8},{10,9... | collective-permute-start | bytes 24584 | tf_op jit(solution)/shard_map/ppermute | solution.py:26
  59.6 78.4 %copy-start = (bf16[2048,2]{0,1:T(2,128)(2,1)S(1)}, bf16[2048,2]{0,1:T(2,128)(2,1)}, u32[]{:S(2)}) copy-start(bf16[2048,2]{0,1:T(2,128)(2,1)} %param.5) | copy-start | bytes 24580
  138.2 7.0 %collective-permute-start.2 = (bf16[2048,2]{0,1:T(2,128)(2,1)S(1)}, bf16[2048,2]{0,1:T(2,128)(2,1)S(1)}, u32[]{:S(2)}, u32[]{:S(2)}) collective-permute-start(bf16[2048,2]{0,1:T(2,128)(2,1)S(1)} %collective-permute-done), channel_id=1, source_target_pairs={{0,1},{1,2},{2,3},{3,4},{4,5},{5,6},{6,7},{7,8},{8,9},{9,10},{10,1... | collective-permute-start | bytes 24584 | tf_op jit(solution)/shard_map/ppermute | solution.py:19
  138.5 6.8 %collective-permute-start.3 = (bf16[2048,2]{0,1:T(2,128)(2,1)S(1)}, bf16[2048,2]{0,1:T(2,128)(2,1)S(1)}, u32[]{:S(2)}, u32[]{:S(2)}) collective-permute-start(bf16[2048,2]{0,1:T(2,128)(2,1)S(1)} %collective-permute-done.1), channel_id=1, source_target_pairs={{0,15},{1,0},{2,1},{3,2},{4,3},{5,4},{6,5},{7,6},{8,7},{9,8},{10,9... | collective-permute-start | bytes 24584 | tf_op jit(solution)/shard_map/ppermute | solution.py:26
  145.3 7.0 %collective-permute-start.4 = (bf16[2048,2]{0,1:T(2,128)(2,1)S(1)}, bf16[2048,2]{0,1:T(2,128)(2,1)S(1)}, u32[]{:S(2)}, u32[]{:S(2)}) collective-permute-start(bf16[2048,2]{0,1:T(2,128)(2,1)S(1)} %collective-permute-done.2), channel_id=1, source_target_pairs={{0,1},{1,2},{2,3},{3,4},{4,5},{5,6},{6,7},{7,8},{8,9},{9,10},{10,1... | collective-permute-start | bytes 24584 | tf_op jit(solution)/shard_map/ppermute | solution.py:19
  145.3 7.0 %collective-permute-start.5 = (bf16[2048,2]{0,1:T(2,128)(2,1)S(1)}, bf16[2048,2]{0,1:T(2,128)(2,1)S(1)}, u32[]{:S(2)}, u32[]{:S(2)}) collective-permute-start(bf16[2048,2]{0,1:T(2,128)(2,1)S(1)} %collective-permute-done.3), channel_id=1, source_target_pairs={{0,15},{1,0},{2,1},{3,2},{4,3},{5,4},{6,5},{7,6},{8,7},{9,8},{10,9... | collective-permute-start | bytes 24584 | tf_op jit(solution)/shard_map/ppermute | solution.py:26
  152.3 7.0 %collective-permute-start.6 = (bf16[2048,2]{0,1:T(2,128)(2,1)S(1)}, bf16[2048,2]{0,1:T(2,128)(2,1)S(1)}, u32[]{:S(2)}, u32[]{:S(2)}) collective-permute-start(bf16[2048,2]{0,1:T(2,128)(2,1)S(1)} %collective-permute-done.4), channel_id=1, source_target_pairs={{0,1},{1,2},{2,3},{3,4},{4,5},{5,6},{6,7},{7,8},{8,9},{9,10},{10,1... | collective-permute-start | bytes 24584 | tf_op jit(solution)/shard_map/ppermute | solution.py:19
  152.3 7.0 %collective-permute-start.7 = (bf16[2048,2]{0,1:T(2,128)(2,1)S(1)}, bf16[2048,2]{0,1:T(2,128)(2,1)S(1)}, u32[]{:S(2)}, u32[]{:S(2)}) collective-permute-start(bf16[2048,2]{0,1:T(2,128)(2,1)S(1)} %collective-permute-done.5), channel_id=1, source_target_pairs={{0,15},{1,0},{2,1},{3,2},{4,3},{5,4},{6,5},{7,6},{8,7},{9,8},{10,9... | collective-permute-start | bytes 24584 | tf_op jit(solution)/shard_map/ppermute | solution.py:26
  159.2 7.0 %collective-permute-start.8 = (bf16[2048,2]{0,1:T(2,128)(2,1)S(1)}, bf16[2048,2]{0,1:T(2,128)(2,1)S(1)}, u32[]{:S(2)}, u32[]{:S(2)}) collective-permute-start(bf16[2048,2]{0,1:T(2,128)(2,1)S(1)} %collective-permute-done.6), channel_id=1, source_target_pairs={{0,1},{1,2},{2,3},{3,4},{4,5},{5,6},{6,7},{7,8},{8,9},{9,10},{10,1... | collective-permute-start | bytes 24584 | tf_op jit(solution)/shard_map/ppermute | solution.py:19
  159.2 7.0 %collective-permute-start.9 = (bf16[2048,2]{0,1:T(2,128)(2,1)S(1)}, bf16[2048,2]{0,1:T(2,128)(2,1)S(1)}, u32[]{:S(2)}, u32[]{:S(2)}) collective-permute-start(bf16[2048,2]{0,1:T(2,128)(2,1)S(1)} %collective-permute-done.7), channel_id=1, source_target_pairs={{0,15},{1,0},{2,1},{3,2},{4,3},{5,4},{6,5},{7,6},{8,7},{9,8},{10,9... | collective-permute-start | bytes 24584 | tf_op jit(solution)/shard_map/ppermute | solution.py:26
  166.2 7.0 %collective-permute-start.10 = (bf16[2048,2]{0,1:T(2,128)(2,1)S(1)}, bf16[2048,2]{0,1:T(2,128)(2,1)S(1)}, u32[]{:S(2)}, u32[]{:S(2)}) collective-permute-start(bf16[2048,2]{0,1:T(2,128)(2,1)S(1)} %collective-permute-done.8), channel_id=1, source_target_pairs={{0,1},{1,2},{2,3},{3,4},{4,5},{5,6},{6,7},{7,8},{8,9},{9,10},{10,1... | collective-permute-start | bytes 24584 | tf_op jit(solution)/shard_map/ppermute | solution.py:19
  166.2 7.0 %collective-permute-start.11 = (bf16[2048,2]{0,1:T(2,128)(2,1)S(1)}, bf16[2048,2]{0,1:T(2,128)(2,1)S(1)}, u32[]{:S(2)}, u32[]{:S(2)}) collective-permute-start(bf16[2048,2]{0,1:T(2,128)(2,1)S(1)} %collective-permute-done.9), channel_id=1, source_target_pairs={{0,15},{1,0},{2,1},{3,2},{4,3},{5,4},{6,5},{7,6},{8,7},{9,8},{10,9... | collective-permute-start | bytes 24584 | tf_op jit(solution)/shard_map/ppermute | solution.py:26
  173.2 7.0 %collective-permute-start.12 = (bf16[2048,2]{0,1:T(2,128)(2,1)S(1)}, bf16[2048,2]{0,1:T(2,128)(2,1)S(1)}, u32[]{:S(2)}, u32[]{:S(2)}) collective-permute-start(bf16[2048,2]{0,1:T(2,128)(2,1)S(1)} %collective-permute-done.10), channel_id=1, source_target_pairs={{0,1},{1,2},{2,3},{3,4},{4,5},{5,6},{6,7},{7,8},{8,9},{9,10},{10,1... | collective-permute-start | bytes 24584 | tf_op jit(solution)/shard_map/ppermute | solution.py:19
  173.2 7.0 %collective-permute-start.13 = (bf16[2048,2]{0,1:T(2,128)(2,1)S(1)}, bf16[2048,2]{0,1:T(2,128)(2,1)S(1)}, u32[]{:S(2)}, u32[]{:S(2)}) collective-permute-start(bf16[2048,2]{0,1:T(2,128)(2,1)S(1)} %collective-permute-done.11), channel_id=1, source_target_pairs={{0,15},{1,0},{2,1},{3,2},{4,3},{5,4},{6,5},{7,6},{8,7},{9,8},{10,9... | collective-permute-start | bytes 24584 | tf_op jit(solution)/shard_map/ppermute | solution.py:26
  180.2 7.0 %collective-permute-start.14 = (bf16[2048,2]{0,1:T(2,128)(2,1)S(1)}, bf16[2048,2]{0,1:T(2,128)(2,1)S(1)}, u32[]{:S(2)}, u32[]{:S(2)}) collective-permute-start(bf16[2048,2]{0,1:T(2,128)(2,1)S(1)} %collective-permute-done.12), channel_id=1, source_target_pairs={{0,1},{1,2},{2,3},{3,4},{4,5},{5,6},{6,7},{7,8},{8,9},{9,10},{10,1... | collective-permute-start | bytes 24584 | tf_op jit(solution)/shard_map/ppermute | solution.py:19
